TPU v7x, 512 devices: a whole 4x8x8 slice. The times are simulated.
512 devices in a mesh: row: 16 (over z, core), col: 32 (over x, y).
Axes of the slice: x: 4, y: 8, z: 8, core: 2. Of those that a mesh axis runs over, the one named last changes fastest.
Arguments:
- trail_adjoint: float32 [16384, 16384], P('row', 'col'), may hold values from -0.046875 to 0.046875
- panel: float32 [16384, 128], P('row', 'col')
- panel_adjoint: float32 [16384, 128], P('row', 'col'), may hold values from -6 to 6
- inv_diag: float32 [128, 128], replicated, as said below
- panel_index: int32 [1], replicated, may hold values from 832 to 895
Outputs:
- panel_grad: float32 [16384, 128], P('row', 'col')
- diag_grad: float32 [128, 128], P(None, 'col')
Inputs may be any that keep to these rules, and one draw needn't show every extreme that they name: inv_diag is lower triangular with a positive diagonal.
All inputs are finite; a program needn't handle non-finite values.
Results may differ from a plain program's by a relative error of at most 0.000075.
Values sent between devices are 32-bit elements; how exact they have to be, the bound alone decides.
No kernel may reach another device: no remote copies, remote signals or barrier semaphores. Data moves between devices by JAX's collectives and lax.ppermute only.
A program may use at most 64 MiB of HBM per device.

v0:
```python
import jax
import jax.numpy as jnp
from jax import lax
from jax.sharding import PartitionSpec as P


def broadcast(value, axis, root):
    mine = lax.axis_index(axis) == root
    return lax.psum(jnp.where(mine, value, jnp.zeros_like(value)), axis)


def body(trail_adjoint, panel, panel_adjoint, inv_diag, panel_index):
    rows_here, thin_cols = panel.shape
    panel_width = inv_diag.shape[0]
    ways_row = lax.axis_size("row")
    ways_col = lax.axis_size("col")
    ways_ratio = ways_col // ways_row
    col_here = lax.axis_index("col")
    index_k = panel_index[0]
    start_mod = jnp.mod(col_here - index_k - 1, ways_col)
    offset = start_mod // ways_row
    col_blocks = rows_here // (panel_width * ways_ratio)
    root_row = jnp.mod(col_here, ways_row)
    panel_rows = lax.all_gather(panel, "col", axis=1, tiled=True)
    shaped = broadcast(panel_rows, "row", root_row).reshape(
        col_blocks, ways_ratio, panel_width, panel_width
    )
    chosen = lax.dynamic_slice_in_dim(shaped, offset, 1, 1)
    column_panel = chosen.reshape(col_blocks * panel_width, panel_width)
    product = jnp.dot(
        trail_adjoint,
        column_panel,
        precision=lax.Precision.HIGHEST,
        preferred_element_type=jnp.float32,
    )
    placed = lax.dynamic_update_slice_in_dim(
        jnp.zeros((rows_here, panel_width), jnp.float32), panel_adjoint, col_here * thin_cols, 1
    )
    local_term = placed - 2.0 * product
    my_inverse = lax.dynamic_slice_in_dim(inv_diag, col_here * thin_cols, thin_cols, 1)
    contract_rows = (((0,), (0,)), ((), ()))
    thin_part = lax.psum_scatter(local_term, "col", scatter_dimension=1, tiled=True)
    full_rows = lax.all_gather(thin_part, "col", axis=1, tiled=True)
    panel_grad = jnp.dot(
        full_rows, my_inverse, precision=lax.Precision.HIGHEST, preferred_element_type=jnp.float32
    )
    gram_local = lax.dot_general(
        full_rows,
        panel,
        contract_rows,
        precision=lax.Precision.HIGHEST,
        preferred_element_type=jnp.float32,
    )
    gram_total = lax.psum(gram_local, "row")
    diag_grad = -lax.dot_general(
        inv_diag,
        gram_total,
        contract_rows,
        precision=lax.Precision.HIGHEST,
        preferred_element_type=jnp.float32,
    )
    return (panel_grad, diag_grad)


def solution(mesh):
    in_specs = (P("row", "col"), P("row", "col"), P("row", "col"), P(), P())
    out_specs = (P("row", "col"), P(None, "col"))
    return jax.shard_map(body, mesh=mesh, in_specs=in_specs, out_specs=out_specs, check_vma=False)
```

profile of v0, /device:TPU:2, one launch (start us, length us, event | category | flops | bytes accessed | tf_op | source)
XLA Modules:
  0.0 444.2 jit_solution(17022918917563937802)
XLA Ops:
  7.2 0.0 copy-start
  7.2 0.0 all-reduce.4.cloned.1.call-start
  7.2 52.3 %all-gather = f32[32,4,1024]{2,1,0:T(4,128)S(1)} all-gather(f32[1,4,1024]{2,1,0:T(4,128)} %bitcast.33), channel_id=1, replica_groups=mesh['row'=16,'col'=32] {'col'}, dimensions={0}, use_global_device_ids=true | all-gather | bytes 540672 | tf_op jit(solution)/shard_map/all_gather | solution.py:24
  59.5 0.1 broadcast_select_fusion
  59.7 0.2 reshape.18
  59.9 1.2 reshape.10
  61.1 0.0 all-reduce.4.cloned.1.call-update
  61.1 0.0 all-reduce.6.cloned.1.call-start
  61.9 0.0 copy-done.3
  62.0 115.0 %all-reduce.4.cloned.1.call-done = f32[4,2,128,128]{2,1,0,3:T(2,128)} async-done(((f32[4,2,128,128]{2,1,0,3:T(2,128)}), f32[4,2,128,128]{2,1,0,3:T(2,128)}) %all-reduce.4.cloned.1.call-update) | async-done | bytes 524304 | tf_op jit(solution)/shard_map/psum | solution.py:9
  177.0 1.9 dynamic-slice_reduce_fusion
  178.8 0.0 copy-done
  178.8 0.0 copy-start.2
  178.9 3.1 fusion.1
  182.0 0.0 all-reduce.6.cloned.1.call-update
  182.0 1.3 dynamic-slice
  183.9 155.1 %all-reduce.6.cloned.1.call-done = f32[1024,128]{0,1:T(8,128)} async-done(((f32[1024,128]{0,1:T(8,128)}), f32[1024,128]{0,1:T(8,128)}) %all-reduce.6.cloned.1.call-update) | async-done | bytes 524304
  339.1 0.8 dynamic-slice_bitcast_fusion
  339.8 48.1 %all-gather.1 = f32[32,4,1024]{2,1,0:T(4,128)S(1)} all-gather(f32[1,4,1024]{2,1,0:T(4,128)S(1)} %dynamic-slice_bitcast_fusion), channel_id=1, replica_groups=mesh['row'=16,'col'=32] {'col'}, dimensions={0}, use_global_device_ids=true | all-gather | bytes 540672 | tf_op jit(solution)/shard_map/all_gather | solution.py:43
  387.9 0.2 reshape.15
  388.1 0.5 fusion.8
  388.6 46.8 %psum.15 = f32[128,4]{1,0:T(8,128)S(1)} all-reduce(f32[128,4]{1,0:T(8,128)S(1)} %fusion.8), channel_id=1, replica_groups=mesh['row'=16,'col'=32] {'row'}, use_global_device_ids=true, to_apply=%region_2.3 | all-reduce | flops 512 | bytes 4096 | tf_op jit(solution)/shard_map/psum | solution.py:54
  435.4 1.0 fusion.5
  436.5 0.8 fusion.2
  (6 shorter events, 0.1 us)
Async XLA Ops:
  7.2 171.7 %copy-start = (f32[1024,512]{1,0:T(8,128)S(1)}, f32[1024,512]{1,0:T(8,128)}, u32[]{:S(2)}) copy-start(f32[1024,512]{1,0:T(8,128)} %param.5) | copy-start | bytes 6291460
  7.2 169.8 %all-reduce.4.cloned.1.call-start = ((), (), s32[]{:S(2)}) async-start(), calls=%async_computation | async-start | bytes 1048576 | tf_op jit(solution)/shard_map/psum | solution.py:9
  59.5 2.4 copy-start.3
  61.1 277.9 %all-reduce.6.cloned.1.call-start = ((), (), s32[]{:S(2)}) async-start(), calls=%async_computation.1 | async-start | bytes 1048576
  178.8 209.2 %copy-start.2 = (f32[1024,4]{0,1:T(4,128)S(1)}, f32[1024,4]{0,1:T(4,128)}, u32[]{:S(2)}) copy-start(f32[1024,4]{0,1:T(4,128)} %param.6) | copy-start | bytes 49156
  182.0 253.5 %copy-start.1 = (f32[128,128]{1,0:T(8,128)S(1)}, f32[128,128]{1,0:T(8,128)}, u32[]{:S(2)}) copy-start(f32[128,128]{1,0:T(8,128)} %param.8) | copy-start | bytes 196612
Sparse Core Ops, SparseCore 0:
  61.3 115.6 all-reduce.3
  182.1 156.9 all-reduce.5
where the time goes:
time: 445 us; the launch traced here: 444 us
  waiting for transfers between devices  270 us (61%)
  blocking collectives  147 us (33%)
  between operations  15.5 us (3%)
  local copies, waits for them, and re-layouts  5.58 us (1%)
  matrix products  5.52 us (1%)
    unnamed x3, waiting for transfers between devices  155 us
    psum x1, waiting for transfers between devices, broadcast(): return lax.psum(jnp.where(mine, value, jnp.zeros_like(value)), axis)  115 us
    all_gather x1, blocking collectives, body(): panel_rows = lax.all_gather(panel, 'col', axis=1, tiled=True)  52.3 us
    all_gather x1, blocking collectives, body(): full_rows = lax.all_gather(thin_part, 'col', axis=1, tiled=True)  48.1 us
    psum x1, blocking collectives, body(): gram_total = lax.psum(gram_local, 'row')  46.8 us
  transfers between devices with their start and end apart: 2, of which 2 were waited for; matrix products, arithmetic and copies ran while one was open for 0% of the time, Pallas kernels for 0%

commit v1 on v0

--- a/solution.py
+++ b/solution.py
@@ -51,7 +51,7 @@
         precision=lax.Precision.HIGHEST,
         preferred_element_type=jnp.float32,
     )
-    gram_total = lax.psum(gram_local, "row")
+    gram_total = jnp.sum(lax.all_gather(gram_local, "row"), axis=0)
     diag_grad = -lax.dot_general(
         inv_diag,
         gram_total,

time: 445 us -> 418 us (0.939)
  the two profiles are of different devices: /device:TPU:2 before, /device:TPU:1 now
where the time goes in v1:
time: 418 us
  waiting for transfers between devices  280 us (67%)
  blocking collectives  111 us (27%)
  between operations  15.5 us (4%)
  local copies, waits for them, and re-layouts  5.58 us (1%)
  matrix products  5.41 us (1%)
    unnamed x3, waiting for transfers between devices  152 us
    psum x1, waiting for transfers between devices, broadcast(): return lax.psum(jnp.where(mine, value, jnp.zeros_like(value)), axis)  128 us
    all_gather x1, blocking collectives, body(): panel_rows = lax.all_gather(panel, 'col', axis=1, tiled=True)  40 us
    all_gather x1, blocking collectives, body(): full_rows = lax.all_gather(thin_part, 'col', axis=1, tiled=True)  36 us
    all_gather x1, blocking collectives, body(): gram_total = jnp.sum(lax.all_gather(gram_local, 'row'), axis=0)  35.1 us
  transfers between devices with their start and end apart: 2, of which 2 were waited for; matrix products, arithmetic and copies ran while one was open for 0% of the time, Pallas kernels for 0%

profile of v1, /device:TPU:1, one launch (start us, length us, event | category | flops | bytes accessed | tf_op | source)
XLA Modules:
  0.0 417.7 jit_solution(14441229577438762019)
XLA Ops:
  7.2 0.0 copy-start
  7.2 0.0 all-reduce.4.cloned.1.call-start
  7.2 40.0 %all-gather.1 = f32[32,4,1024]{2,1,0:T(4,128)S(1)} all-gather(f32[1,4,1024]{2,1,0:T(4,128)} %bitcast.39), channel_id=1, replica_groups=mesh['row'=16,'col'=32] {'col'}, dimensions={0}, use_global_device_ids=true | all-gather | bytes 540672 | tf_op jit(solution)/shard_map/all_gather | solution.py:24
  47.2 0.1 broadcast_select_fusion
  47.3 0.2 reshape.19
  47.5 1.2 reshape.10
  48.8 0.0 all-reduce.4.cloned.1.call-update
  48.8 0.0 all-reduce.6.cloned.1.call-start
  49.6 0.0 copy-done.3
  49.6 128.2 %all-reduce.4.cloned.1.call-done = f32[4,2,128,128]{2,1,0,3:T(2,128)} async-done(((f32[4,2,128,128]{2,1,0,3:T(2,128)}), f32[4,2,128,128]{2,1,0,3:T(2,128)}) %all-reduce.4.cloned.1.call-update) | async-done | bytes 524304 | tf_op jit(solution)/shard_map/psum | solution.py:9
  177.8 1.9 dynamic-slice_reduce_fusion
  179.6 0.0 copy-done
  179.7 0.0 copy-start.2
  179.7 3.1 fusion.1
  182.8 0.0 all-reduce.6.cloned.1.call-update
  182.8 1.3 dynamic-slice
  184.7 151.8 %all-reduce.6.cloned.1.call-done = f32[1024,128]{0,1:T(8,128)} async-done(((f32[1024,128]{0,1:T(8,128)}), f32[1024,128]{0,1:T(8,128)}) %all-reduce.6.cloned.1.call-update) | async-done | bytes 524304
  336.5 0.8 dynamic-slice_bitcast_fusion
  337.3 36.0 %all-gather.2 = f32[32,4,1024]{2,1,0:T(4,128)S(1)} all-gather(f32[1,4,1024]{2,1,0:T(4,128)S(1)} %dynamic-slice_bitcast_fusion), channel_id=1, replica_groups=mesh['row'=16,'col'=32] {'col'}, dimensions={0}, use_global_device_ids=true | all-gather | bytes 540672 | tf_op jit(solution)/shard_map/all_gather | solution.py:43
  373.2 0.2 reshape.16
  373.4 0.5 fusion.8
  373.9 35.1 %all-gather = f32[2048,4]{0,1:T(4,128)S(1)} all-gather(f32[128,4]{0,1:T(4,128)S(1)} %fusion.8), channel_id=2, replica_groups=mesh['row'=16,'col'=32] {'row'}, dimensions={0}, use_global_device_ids=true | all-gather | bytes 34816 | tf_op jit(solution)/shard_map/all_gather | solution.py:54
  409.1 1.1 fusion.5
  410.1 0.7 fusion.2
  (7 shorter events, 0.1 us)
Async XLA Ops:
  7.2 172.5 %copy-start = (f32[1024,512]{1,0:T(8,128)S(1)}, f32[1024,512]{1,0:T(8,128)}, u32[]{:S(2)}) copy-start(f32[1024,512]{1,0:T(8,128)} %param.5) | copy-start | bytes 6291460
  7.2 170.6 %all-reduce.4.cloned.1.call-start = ((), (), s32[]{:S(2)}) async-start(), calls=%async_computation | async-start | bytes 1048576 | tf_op jit(solution)/shard_map/psum | solution.py:9
  47.2 2.4 copy-start.3
  48.8 287.7 %all-reduce.6.cloned.1.call-start = ((), (), s32[]{:S(2)}) async-start(), calls=%async_computation.1 | async-start | bytes 1048576
  179.7 193.8 %copy-start.2 = (f32[1024,4]{0,1:T(4,128)S(1)}, f32[1024,4]{0,1:T(4,128)}, u32[]{:S(2)}) copy-start(f32[1024,4]{0,1:T(4,128)} %param.6) | copy-start | bytes 49156
  182.8 226.3 %copy-start.1 = (f32[128,128]{1,0:T(8,128)S(1)}, f32[128,128]{1,0:T(8,128)}, u32[]{:S(2)}) copy-start(f32[128,128]{1,0:T(8,128)} %param.8) | copy-start | bytes 196612
Sparse Core Ops, SparseCore 0:
  48.9 128.8 all-reduce.3
  182.9 153.5 all-reduce.5
